TPU v7x, 256 devices: a whole 4x4x8 slice. The times are simulated.
256 devices in a mesh: wave: 8 (over z_hi, core), brick: 32 (over z_lo, x, y).
Axes of the slice: x: 4, y: 4, z: 8 (z_hi: 4, z_lo: 2; z = z_hi * 2 + z_lo), core: 2. Of those that a mesh axis runs over, the one named last changes fastest.
Arguments:
- sources: float32 [8, 6, 256, 6, 4096], P('wave', None, 'brick'), may hold values from -6 to 6
- permittivity: float32 [256, 6, 4096], P('brick'), may hold values from 1 to 4
- wave_number_sq: float32 [8], P('wave'), may hold values from 0.5 to 3
- pixel_list: int32 [32, 256], P('brick'), may hold values from 0 to 255, each once within a row
Outputs:
- design_grad: float32 [32, 32768], P('brick')
Inputs may be any that keep to these rules, and one draw needn't show every extreme that they name: `pixel_list`: each row is a permutation of 0 to 255.
All inputs are finite; a program needn't handle non-finite values.
Results may differ from a plain program's by a relative error of at most 0.0001.
Values sent between devices are 32-bit elements; how exact they have to be, the bound alone decides.
A program may use at most 128 MiB of HBM per device.

v0:
```python
import jax
import jax.numpy as jnp
from jax import lax
from jax.sharding import PartitionSpec as P

SWEEPS = 3
RADIUS = 2
RUN = 128


RELAX = 0.5


def padded_2(x, sides, width):
    for axis, dim in sides:
        peers, length = (lax.axis_size(axis), x.shape[dim])
        up = [(i, (i + 1) % peers) for i in range(peers - 1)]
        down = [(j, i) for i, j in up]
        last = lax.slice_in_dim(x, length - width, length, axis=dim)
        initial = lax.slice_in_dim(x, 0, width, axis=dim)
        before = lax.ppermute(last, axis, up)
        after = lax.ppermute(initial, axis, down)
        x = jnp.concatenate([before, x, after], axis=dim)
    return x


def ahead_x(values):
    return values[..., 1:, :, :] - values[..., :-1, :, :]


def ahead_y(values):
    return jnp.concatenate([values[..., 1:], jnp.zeros_like(values[..., :1])], -1) - values


def ahead_z(values):
    return jnp.concatenate([values[..., 1:, :], jnp.zeros_like(values[..., :1, :])], -2) - values


def behind_y(values):
    return values - jnp.concatenate([jnp.zeros_like(values[..., :1]), values[..., :-1]], -1)


def behind_z(values):
    return values - jnp.concatenate([jnp.zeros_like(values[..., :1, :]), values[..., :-1, :]], -2)


def curl_curl(padded):
    comp_x = padded[..., 0, :, :, :]
    comp_y = padded[..., 1, :, :, :]
    comp_z = padded[..., 2, :, :, :]
    lead_x = comp_x[..., :-1, :, :]
    lead_y = comp_y[..., :-1, :, :]
    lead_z = comp_z[..., :-1, :, :]
    mag_x = ahead_y(lead_z) - ahead_z(lead_y)
    mag_y = ahead_z(lead_x) - ahead_x(comp_z)
    mag_z = ahead_x(comp_y) - ahead_y(lead_x)
    curl_x = behind_y(mag_z[..., 1:, :, :]) - behind_z(mag_y[..., 1:, :, :])
    curl_y = behind_z(mag_x[..., 1:, :, :]) - ahead_x(mag_z)
    curl_z = ahead_x(mag_y) - behind_y(mag_x[..., 1:, :, :])
    return jnp.stack([curl_x, curl_y, curl_z], -4)


def relax_step(fields, padded, drive_all, permit, wave_sq, diagonal):
    return fields + RELAX * (drive_all - curl_curl(padded) - wave_sq * permit * fields) / diagonal


def smooth_padded(padded, length, along):
    summed = jnp.zeros_like(lax.slice_in_dim(padded, 0, length, axis=along))
    for offset in range(2 * RADIUS + 1):
        weight = (RADIUS + 1 - abs(offset - RADIUS)) / (RADIUS + 1) ** 2
        summed = summed + weight * lax.slice_in_dim(padded, offset, offset + length, axis=along)
    return summed


def pick_runs(smooth, order):
    blocks = smooth.reshape(-1, RUN)
    return jnp.take(blocks, order, axis=0).reshape(1, -1)


def on_device(sources, permittivity, wave_number_sq, pixel_list):
    wave_sq = wave_number_sq[0]
    brick_rows = permittivity.shape[0]
    layers = permittivity.shape[1]
    columns = permittivity.shape[2]
    drive_all = sources[0].reshape(2, 3, brick_rows, layers, columns)
    diagonal = 4.0 + wave_sq * permittivity
    fields = RELAX * drive_all / diagonal
    for sweep_index in range(SWEEPS - 1):
        padded = padded_2(fields, (("brick", 2),), 1)
        fields = relax_step(fields, padded, drive_all, permittivity, wave_sq, diagonal)
    density = -wave_sq * jnp.sum(fields[0] * fields[1], axis=(0, 2))
    row_sum = lax.psum(density, "wave")
    along_y = smooth_padded(jnp.pad(row_sum, ((0, 0), (RADIUS, RADIUS))), columns, 1)
    widened_rows = padded_2(along_y, (("brick", 0),), RADIUS)
    smooth = smooth_padded(widened_rows, brick_rows, 0)
    return pick_runs(smooth, pixel_list[0])


def solution(mesh):
    return jax.shard_map(
        on_device,
        mesh=mesh,
        in_specs=(
            P("wave", None, "brick", None, None),
            P("brick", None, None),
            P("wave"),
            P("brick", None),
        ),
        out_specs=P("brick", None),
        check_vma=False,
    )
```

profile of v0, /device:TPU:30, one launch (start us, length us, event | category | flops | bytes accessed | tf_op | source)
XLA Modules:
  0.0 236.2 jit_solution(8491026144020708894)
XLA Ops:
  10.3 3.0 %multiply_divide_fusion = f32[2,3,8,6,4096]{4,2,3,1,0:T(8,128)S(1)} fusion(f32[2,3,8,6,4096]{4,2,3,1,0:T(8,128)} %bitcast.41, f32[8,6,4096]{2,0,1:T(8,128)S(1)} %get-tuple-element.5), kind=kLoop, calls=%fused_computation.14 | loop fusion | flops 2359296 | bytes 10223616 | tf_op jit(solution)/shard_map/div | solution.py:87
  14.5 3.4 %collective-permute-start = (f32[2,3,1,6,4096]{4,2,3,1,0:T(1,128)S(1)}, f32[2,3,1,6,4096]{4,2,3,1,0:T(1,128)S(1)}, u32[]{:S(2)}, u32[]{:S(2)}) collective-permute-start(f32[2,3,1,6,4096]{4,2,3,1,0:T(1,128)S(1)} %get-tuple-element.15), channel_id=1, source_target_pairs={{0,1},{1,2},{2,3},{3,4},{4,5},{5,6},{6,7},{7,8},{8,9},{9,10},{10,1... | collective-permute-start | bytes 1769480 | tf_op jit(solution)/shard_map/ppermute | solution.py:21
  17.9 2.4 %collective-permute-start.1 = (f32[2,3,1,6,4096]{4,2,3,1,0:T(1,128)S(1)}, f32[2,3,1,6,4096]{4,2,3,1,0:T(1,128)S(1)}, u32[]{:S(2)}, u32[]{:S(2)}) collective-permute-start(f32[2,3,1,6,4096]{4,2,3,1,0:T(1,128)S(1)} %get-tuple-element.16), channel_id=1, source_target_pairs={{1,0},{2,1},{3,2},{4,3},{5,4},{6,5},{7,6},{8,7},{9,8},{10,9},{11,1... | collective-permute-start | bytes 1769480 | tf_op jit(solution)/shard_map/ppermute | solution.py:22
  20.3 11.1 %collective-permute-done = f32[2,3,1,6,4096]{4,2,3,1,0:T(1,128)S(1)} collective-permute-done((f32[2,3,1,6,4096]{4,2,3,1,0:T(1,128)S(1)}, f32[2,3,1,6,4096]{4,2,3,1,0:T(1,128)S(1)}, u32[]{:S(2)}, u32[]{:S(2)}) %collective-permute-start) | collective-permute-done | bytes 589856 | tf_op jit(solution)/shard_map/ppermute | solution.py:21
  31.4 7.3 %collective-permute-done.1 = f32[2,3,1,6,4096]{4,2,3,1,0:T(1,128)S(1)} collective-permute-done((f32[2,3,1,6,4096]{4,2,3,1,0:T(1,128)S(1)}, f32[2,3,1,6,4096]{4,2,3,1,0:T(1,128)S(1)}, u32[]{:S(2)}, u32[]{:S(2)}) %collective-permute-start.1) | collective-permute-done | bytes 589856 | tf_op jit(solution)/shard_map/ppermute | solution.py:22
  44.3 2.6 %slice.281 = f32[2,9,6,4095]{3,1,2,0:T(8,128)} slice(f32[2,10,6,4096]{3,1,2,0:T(8,128)S(1)} %get-tuple-element.11), slice={[0:2], [0:9], [0:6], [1:4096]} | slice | bytes 3538080 | tf_op jit(solution)/shard_map/slice | solution.py:32
  48.6 5.7 %fusion.10 = (f32[2,9,6,4096]{3,1,2,0:T(8,128)S(1)}, f32[2,9,6,4096]{3,1,2,0:T(8,128)}, f32[2,9,6,4096]{3,1,2,0:T(8,128)S(1)}) fusion(f32[2,10,6,4096]{3,1,2,0:T(8,128)S(1)} %get-tuple-element.10, f32[2,9,6,4095]{3,1,2,0:T(8,128)S(1)} %slice.271, f32[2,10,6,4096]{3,1,2,0:T(8,128)S(1)} %get-tuple-element.12, f32[2,10,6,4096]{3,1,2,0:T(8,128)S(1)} %get-tuple-element.11, ...), kind=kLoop, calls=%fused_computation.27 | loop fusion | flops 3981312 | bytes 20642976 | tf_op jit(solution)/shard_map/sub | solution.py:56
  58.4 3.1 %slice.280 = f32[2,8,5,4096]{3,1,2,0:T(8,128)} slice(f32[2,9,6,4096]{3,1,2,0:T(8,128)} %get-tuple-element.27), slice={[0:2], [1:9], [0:5], [0:4096]} | slice | bytes 2621440 | tf_op jit(solution)/shard_map/slice | solution.py:44
  61.5 8.6 %subtract_bitcast_fusion.1 = (f32[2,1,8,6,4096]{4,2,3,0,1:T(8,128)S(1)}, f32[2,1,8,6,4096]{4,2,3,0,1:T(8,128)}, f32[2,1,8,6,4096]{4,2,3,0,1:T(8,128)}) fusion(f32[2,8,5,4096]{3,1,2,0:T(8,128)} %slice.280, f32[2,8,6,4095]{3,1,2,0:T(8,128)} %slice.274, f32[2,9,6,4096]{3,1,2,0:T(8,128)} %get-tuple-element.27, f32[2,9,6,4096]{3,1,2,0:T(8,128)S(1)} %get-tuple-element.26, ...), kind=kLoop, calls=%fused_computation.46 | loop fusion | flops 3538944 | bytes 18349312 | tf_op jit(solution)/shard_map/stack | solution.py:60
  70.2 4.3 %fusion.6 = f32[2,3,8,6,4096]{4,2,3,1,0:T(8,128)S(1)} fusion(f32[8,6,4096]{2,0,1:T(8,128)} %get-tuple-element.6, f32[8,6,4096]{2,0,1:T(8,128)} %copy-done.5, f32[2,3,8,6,4096]{4,2,3,1,0:T(8,128)S(1)} %bitcast.44, f32[2,1,8,6,4096]{4,2,3,0,1:T(8,128)} %get-tuple-element.25, f32[2,1,8,6,4096]{4,2,3,0,1:T(8,128)} %get-tuple-element.24, ...), kind=kLoop, calls=%fused_computation.13 | loop fusion | flops 11796480 | bytes 15728640 | tf_op jit(solution)/shard_map/add | solution.py:64
  74.5 2.2 copy-done
  79.9 4.1 %collective-permute-start.3 = (f32[2,3,1,6,4096]{4,2,3,1,0:T(1,128)S(1)}, f32[2,3,1,6,4096]{4,2,3,1,0:T(1,128)}, u32[]{:S(2)}, u32[]{:S(2)}) collective-permute-start(f32[2,3,1,6,4096]{4,2,3,1,0:T(1,128)S(1)} %get-tuple-element.14), channel_id=1, source_target_pairs={{1,0},{2,1},{3,2},{4,3},{5,4},{6,5},{7,6},{8,7},{9,8},{10,9},{11,1... | collective-permute-start | bytes 1769480 | tf_op jit(solution)/shard_map/ppermute | solution.py:22
  84.0 9.7 %collective-permute-done.2 = f32[2,3,1,6,4096]{4,2,3,1,0:T(1,128)S(1)} collective-permute-done((f32[2,3,1,6,4096]{4,2,3,1,0:T(1,128)S(1)}, f32[2,3,1,6,4096]{4,2,3,1,0:T(1,128)S(1)}, u32[]{:S(2)}, u32[]{:S(2)}) %collective-permute-start.2) | collective-permute-done | bytes 589856 | tf_op jit(solution)/shard_map/ppermute | solution.py:21
  94.5 5.4 %collective-permute-done.3 = f32[2,3,1,6,4096]{4,2,3,1,0:T(1,128)} collective-permute-done((f32[2,3,1,6,4096]{4,2,3,1,0:T(1,128)S(1)}, f32[2,3,1,6,4096]{4,2,3,1,0:T(1,128)}, u32[]{:S(2)}, u32[]{:S(2)}) %collective-permute-start.3) | collective-permute-done | bytes 589856 | tf_op jit(solution)/shard_map/ppermute | solution.py:22
  100.0 3.5 %pad_maximum_fusion.1 = f32[2,3,10,6,4096]{4,2,3,1,0:T(8,128)S(1)} fusion(f32[2,3,1,6,4096]{4,2,3,1,0:T(1,128)} %collective-permute-done.3, f32[2,3,8,6,4096]{4,2,3,1,0:T(8,128)} %copy-done, f32[2,3,1,6,4096]{4,2,3,1,0:T(1,128)} %copy-done.6), kind=kLoop, calls=%fused_computation.2 | loop fusion | flops 2949120 | bytes 11796480 | tf_op jit(solution)/shard_map/concatenate | solution.py:23
  107.2 2.6 %slice.304 = f32[2,9,6,4095]{3,1,2,0:T(8,128)} slice(f32[2,10,6,4096]{3,1,2,0:T(8,128)S(1)} %get-tuple-element.8), slice={[0:2], [0:9], [0:6], [1:4096]} | slice | bytes 3538080 | tf_op jit(solution)/shard_map/slice | solution.py:32
  111.4 5.7 %fusion.8 = (f32[2,9,6,4096]{3,1,2,0:T(8,128)S(1)}, f32[2,9,6,4096]{3,1,2,0:T(8,128)}, f32[2,9,6,4096]{3,1,2,0:T(8,128)S(1)}) fusion(f32[2,10,6,4096]{3,1,2,0:T(8,128)S(1)} %get-tuple-element.7, f32[2,9,6,4095]{3,1,2,0:T(8,128)S(1)} %slice.294, f32[2,10,6,4096]{3,1,2,0:T(8,128)S(1)} %get-tuple-element.9, f32[2,10,6,4096]{3,1,2,0:T(8,128)S(1)} %get-tuple-element.8, ...), kind=kLoop, calls=%fused_computation.20 | loop fusion | flops 3981312 | bytes 20642976 | tf_op jit(solution)/shard_map/sub | solution.py:56
  121.3 3.1 %slice.303 = f32[2,8,5,4096]{3,1,2,0:T(8,128)} slice(f32[2,9,6,4096]{3,1,2,0:T(8,128)} %get-tuple-element.21), slice={[0:2], [1:9], [0:5], [0:4096]} | slice | bytes 2621440 | tf_op jit(solution)/shard_map/slice | solution.py:44
  124.4 9.2 %subtract_bitcast_fusion = (f32[2,1,8,6,4096]{4,2,3,0,1:T(8,128)}, f32[2,1,8,6,4096]{4,2,3,0,1:T(8,128)}, f32[2,1,8,6,4096]{4,2,3,0,1:T(8,128)}) fusion(f32[2,8,5,4096]{3,1,2,0:T(8,128)} %slice.303, f32[2,8,6,4095]{3,1,2,0:T(8,128)} %slice.297, f32[2,9,6,4096]{3,1,2,0:T(8,128)} %get-tuple-element.21, f32[2,9,6,4096]{3,1,2,0:T(8,128)S(1)} %get-tuple-element.20, ...), kind=kLoop, calls=%fused_computation.45 | loop fusion | flops 3538944 | bytes 18349312 | tf_op jit(solution)/shard_map/stack | solution.py:60
  133.7 5.5 %fusion.3 = f32[2,3,8,6,4096]{4,2,3,1,0:T(8,128)S(1)} fusion(f32[2,3,8,6,4096]{4,2,3,1,0:T(8,128)S(1)} %bitcast.47, f32[8,6,4096]{2,0,1:T(8,128)} %get-tuple-element.6, f32[8,6,4096]{2,0,1:T(8,128)} %copy-done.5, f32[2,1,8,6,4096]{4,2,3,0,1:T(8,128)} %get-tuple-element.19, f32[2,1,8,6,4096]{4,2,3,0,1:T(8,128)} %get-tuple-element.18, ...), kind=kLoop, calls=%fused_computation.9 | loop fusion | flops 21233664 | bytes 20447232 | tf_op jit(solution)/shard_map/add | solution.py:64
  140.1 73.5 %all-reduce.19.cloned.1.call-done = f32[8,4096]{1,0:T(8,128)} async-done(((f32[8,4096]{1,0:T(8,128)}), f32[8,4096]{1,0:T(8,128)}) %all-reduce.19.cloned.1.call-update) | async-done | bytes 131088 | tf_op jit(solution)/shard_map/psum | solution.py:92
  215.2 2.5 %collective-permute-start.4 = (f32[2,4096]{1,0:T(2,128)S(1)}, f32[2,4096]{1,0:T(2,128)S(1)}, u32[]{:S(2)}, u32[]{:S(2)}) collective-permute-start(f32[2,4096]{1,0:T(2,128)S(1)} %get-tuple-element.29), channel_id=1, source_target_pairs={{0,1},{1,2},{2,3},{3,4},{4,5},{5,6},{6,7},{7,8},{8,9},{9,10},{10,1... | collective-permute-start | bytes 98312 | tf_op jit(solution)/shard_map/ppermute | solution.py:21
  217.7 3.4 %collective-permute-start.5 = (f32[2,4096]{1,0:T(2,128)S(1)}, f32[2,4096]{1,0:T(2,128)S(1)}, u32[]{:S(2)}, u32[]{:S(2)}) collective-permute-start(f32[2,4096]{1,0:T(2,128)S(1)} %get-tuple-element.30), channel_id=1, source_target_pairs={{1,0},{2,1},{3,2},{4,3},{5,4},{6,5},{7,6},{8,7},{9,8},{10,9},{11,1... | collective-permute-start | bytes 98312 | tf_op jit(solution)/shard_map/ppermute | solution.py:22
  221.1 6.6 %collective-permute-done.5 = f32[2,4096]{1,0:T(2,128)S(1)} collective-permute-done((f32[2,4096]{1,0:T(2,128)S(1)}, f32[2,4096]{1,0:T(2,128)S(1)}, u32[]{:S(2)}, u32[]{:S(2)}) %collective-permute-start.5) | collective-permute-done | bytes 32800 | tf_op jit(solution)/shard_map/ppermute | solution.py:22
  (58 shorter events, 33.2 us)
Async XLA Ops:
  6.5 207.1 %all-reduce.19.cloned.1.call-start = ((), (), s32[]{:S(2)}) async-start(), calls=%async_computation | async-start | bytes 262144 | tf_op jit(solution)/shard_map/psum | solution.py:92
  9.3 0.9 copy-start.5
  14.5 17.0 %collective-permute-start = (f32[2,3,1,6,4096]{4,2,3,1,0:T(1,128)S(1)}, f32[2,3,1,6,4096]{4,2,3,1,0:T(1,128)S(1)}, u32[]{:S(2)}, u32[]{:S(2)}) collective-permute-start(f32[2,3,1,6,4096]{4,2,3,1,0:T(1,128)S(1)} %get-tuple-element.15), channel_id=1, source_target_pairs={{0,1},{1,2},{2,3},{3,4},{4,5},{5,6},{6,7},{7,8},{8,9},{9,10},{10,1... | collective-permute-start | bytes 1769480 | tf_op jit(solution)/shard_map/ppermute | solution.py:21
  17.9 20.9 %collective-permute-start.1 = (f32[2,3,1,6,4096]{4,2,3,1,0:T(1,128)S(1)}, f32[2,3,1,6,4096]{4,2,3,1,0:T(1,128)S(1)}, u32[]{:S(2)}, u32[]{:S(2)}) collective-permute-start(f32[2,3,1,6,4096]{4,2,3,1,0:T(1,128)S(1)} %get-tuple-element.16), channel_id=1, source_target_pairs={{1,0},{2,1},{3,2},{4,3},{5,4},{6,5},{7,6},{8,7},{9,8},{10,9},{11,1... | collective-permute-start | bytes 1769480 | tf_op jit(solution)/shard_map/ppermute | solution.py:22
  54.3 4.1 %copy-start.1 = (f32[2,9,6,4096]{3,1,2,0:T(8,128)}, f32[2,9,6,4096]{3,1,2,0:T(8,128)S(1)}, u32[]{:S(2)}) copy-start(f32[2,9,6,4096]{3,1,2,0:T(8,128)S(1)} %get-tuple-element.28) | copy-start | bytes 5308420
  58.4 11.7 %slice-start = ((s8[4718592]{0:T(1024)(128)(4,1)}), s8[4194304]{0:T(1024)(128)(4,1)S(1)}, s32[]{:S(2)}) async-start(s8[4718592]{0:T(1024)(128)(4,1)} %bitcast.42), calls=%async_computation.1 | async-start | bytes 8388608
  61.5 8.7 %slice-start.1 = ((s8[4718592]{0:T(1024)(128)(4,1)}), s8[524288]{0:T(1024)(128)(4,1)S(1)}, s32[]{:S(2)}) async-start(s8[4718592]{0:T(1024)(128)(4,1)} %bitcast.42), calls=%async_computation.2 | async-start | bytes 1048576
  70.1 4.3 %copy-start.3 = (f32[2,1,8,6,4096]{4,2,3,0,1:T(8,128)}, f32[2,1,8,6,4096]{4,2,3,0,1:T(8,128)S(1)}, u32[]{:S(2)}) copy-start(f32[2,1,8,6,4096]{4,2,3,0,1:T(8,128)S(1)} %get-tuple-element.23) | copy-start | bytes 4718596
  70.2 13.8 %copy-start.7 = (s32[1,256]{1,0:T(1,128)S(1)}, s32[1,256]{1,0:T(1,128)}, u32[]{:S(2)}) copy-start(s32[1,256]{1,0:T(1,128)} %param.7) | copy-start | bytes 3076
  74.4 2.2 copy-start
  77.9 15.8 %collective-permute-start.2 = (f32[2,3,1,6,4096]{4,2,3,1,0:T(1,128)S(1)}, f32[2,3,1,6,4096]{4,2,3,1,0:T(1,128)S(1)}, u32[]{:S(2)}, u32[]{:S(2)}) collective-permute-start(f32[2,3,1,6,4096]{4,2,3,1,0:T(1,128)S(1)} %get-tuple-element.13), channel_id=1, source_target_pairs={{0,1},{1,2},{2,3},{3,4},{4,5},{5,6},{6,7},{7,8},{8,9},{9,10},{10,1... | collective-permute-start | bytes 1769480 | tf_op jit(solution)/shard_map/ppermute | solution.py:21
  79.9 20.1 %collective-permute-start.3 = (f32[2,3,1,6,4096]{4,2,3,1,0:T(1,128)S(1)}, f32[2,3,1,6,4096]{4,2,3,1,0:T(1,128)}, u32[]{:S(2)}, u32[]{:S(2)}) collective-permute-start(f32[2,3,1,6,4096]{4,2,3,1,0:T(1,128)S(1)} %get-tuple-element.14), channel_id=1, source_target_pairs={{1,0},{2,1},{3,2},{4,3},{5,4},{6,5},{7,6},{8,7},{9,8},{10,9},{11,1... | collective-permute-start | bytes 1769480 | tf_op jit(solution)/shard_map/ppermute | solution.py:22
  93.7 0.8 copy-start.6
  117.2 4.1 %copy-start.2 = (f32[2,9,6,4096]{3,1,2,0:T(8,128)}, f32[2,9,6,4096]{3,1,2,0:T(8,128)S(1)}, u32[]{:S(2)}) copy-start(f32[2,9,6,4096]{3,1,2,0:T(8,128)S(1)} %get-tuple-element.22) | copy-start | bytes 5308420
  121.3 12.3 %slice-start.2 = ((s8[4718592]{0:T(1024)(128)(4,1)}), s8[4194304]{0:T(1024)(128)(4,1)S(1)}, s32[]{:S(2)}) async-start(s8[4718592]{0:T(1024)(128)(4,1)} %bitcast.45), calls=%async_computation.3 | async-start | bytes 8388608
  124.4 9.3 %slice-start.3 = ((s8[4718592]{0:T(1024)(128)(4,1)}), s8[524288]{0:T(1024)(128)(4,1)S(1)}, s32[]{:S(2)}) async-start(s8[4718592]{0:T(1024)(128)(4,1)} %bitcast.45), calls=%async_computation.4 | async-start | bytes 1048576
  124.4 9.3 %copy-start.4 = (f32[2,1,8,6,4096]{4,2,3,0,1:T(8,128)S(1)}, f32[2,1,8,6,4096]{4,2,3,0,1:T(8,128)}, u32[]{:S(2)}) copy-start(f32[2,1,8,6,4096]{4,2,3,0,1:T(8,128)} %copy-done.3) | copy-start | bytes 4718596
  215.2 5.9 %collective-permute-start.4 = (f32[2,4096]{1,0:T(2,128)S(1)}, f32[2,4096]{1,0:T(2,128)S(1)}, u32[]{:S(2)}, u32[]{:S(2)}) collective-permute-start(f32[2,4096]{1,0:T(2,128)S(1)} %get-tuple-element.29), channel_id=1, source_target_pairs={{0,1},{1,2},{2,3},{3,4},{4,5},{5,6},{6,7},{7,8},{8,9},{9,10},{10,1... | collective-permute-start | bytes 98312 | tf_op jit(solution)/shard_map/ppermute | solution.py:21
  217.7 10.0 %collective-permute-start.5 = (f32[2,4096]{1,0:T(2,128)S(1)}, f32[2,4096]{1,0:T(2,128)S(1)}, u32[]{:S(2)}, u32[]{:S(2)}) collective-permute-start(f32[2,4096]{1,0:T(2,128)S(1)} %get-tuple-element.30), channel_id=1, source_target_pairs={{1,0},{2,1},{3,2},{4,3},{5,4},{6,5},{7,6},{8,7},{9,8},{10,9},{11,1... | collective-permute-start | bytes 98312 | tf_op jit(solution)/shard_map/ppermute | solution.py:22
Sparse Core Ops, SparseCore 0:
  140.2 73.3 all-reduce.18
where the time goes:
time: 237 us; the launch traced here: 236 us
  waiting for transfers between devices  114 us (48%)
  other arithmetic  52.8 us (22%)
  local copies, waits for them, and re-layouts  37.7 us (16%)
  starting transfers between devices  17.7 us (7%)
  between operations  14.3 us (6%)
    psum x1, waiting for transfers between devices, on_device(): row_sum = lax.psum(density, 'wave')  73.5 us
    ppermute x3, waiting for transfers between devices, padded_2(): before = lax.ppermute(last, axis, up)  20.8 us
    ppermute x3, waiting for transfers between devices, padded_2(): after = lax.ppermute(initial, axis, down)  19.4 us
    another operation x2, other arithmetic, curl_curl(): return jnp.stack([curl_x, curl_y, curl_z], -4)  17.9 us
    sub x2, other arithmetic, curl_curl(): mag_z = ahead_x(comp_y) - ahead_y(lead_x)  11.5 us
    ppermute x3, starting transfers between devices, padded_2(): after = lax.ppermute(initial, axis, down)  9.93 us
    add x2, other arithmetic, relax_step(): fields + RELAX * (drive_all - curl_curl(padded) - wave_sq * permit * fiel...  9.77 us
    slice x4, local copies, waits for them, and re-layouts, behind_z(): values[..., :-1, :]  8.64 us
  transfers between devices with their start and end apart: 7, of which 6 were waited for; matrix products, arithmetic and copies ran while one was open for 0% of the time, Pallas kernels for 0%

commit v1 on v0

v1 whole, which is shorter than its diff:
```python
import functools

import jax
import jax.numpy as jnp
from jax import lax
from jax.experimental import pallas as pl
from jax.experimental.pallas import tpu as pltpu
from jax.sharding import PartitionSpec as P

RADIUS = 2
RUN = 128
LANES = 128
MESH = pl.DeviceIdType.MESH
WEIGHTS = [(RADIUS + 1 - abs(d)) / (RADIUS + 1) ** 2 for d in range(RADIUS + 1)]


def columns_of(start, count):
    return pl.ds(start * LANES, count * LANES)


def block_at(j):
    return pl.ds(pl.multiple_of(j * LANES, LANES), LANES)


def windows(blocks, chunks, lag):
    per = blocks // chunks
    starts = [max(per * c - lag, 0) for c in range(chunks)] + [blocks]
    return list(zip(starts[:-1], starts[1:]))


def body(
    n_wave, n_brick, blocks, layers, chunks,
    wave_ref, pixel_ref, src, eps, out_ref,
    drive, permit, ratio, first, carry,
    out_left, out_right, in_left, in_right,
    density, edge_top, edge_bottom, parts, from_left, from_right, rows, whole, runs,
    load_sem, halo_send, halo_recv, part_send, part_recv, edge_send, edge_recv, gather_send, gather_recv,
):
    wave = lax.axis_index("wave")
    brick = lax.axis_index("brick")
    after = lax.rem(brick + 1, n_brick)
    before = lax.rem(brick + n_brick - 1, n_brick)
    peers = [lax.rem(wave + p, n_wave) for p in range(n_wave)]
    owned = blocks // n_wave
    fields = 3 * layers

    loads = []
    per = blocks // chunks
    for c in range(chunks):
        at = columns_of(per * c, per)
        pair = (
            pltpu.make_async_copy(eps.at[:, :, at], permit.at[:, :, at], load_sem.at[0, c]),
            pltpu.make_async_copy(src.at[:, :, at], drive.at[:, :, at], load_sem.at[1, c]),
        )
        for copy in pair:
            copy.start()
        loads.append(pair)

    barrier = pltpu.get_barrier_semaphore()
    for p in range(n_wave):
        if p:
            pl.semaphore_signal(barrier, inc=1, device_id=(peers[p], brick), device_id_type=MESH)
        for side in (before, after):
            pl.semaphore_signal(barrier, inc=1, device_id=(peers[p], side), device_id_type=MESH)

    wave_sq = wave_ref[0]
    lane = lax.broadcasted_iota(jnp.int32, (8, LANES), 1)
    row = lax.broadcasted_iota(jnp.int32, (8, LANES), 0)
    first_lane, last_lane = lane == 0, lane == LANES - 1
    first_row, last_row = row == 0, row == 7
    edge = columns_of(blocks, 1)
    nothing = jnp.zeros((8, LANES), jnp.float32)
    for plane in range(2 * fields):
        drive[plane, :, edge] = nothing
        first[plane, :, edge] = nothing
    for z in range(layers):
        ratio[z, :, edge] = nothing
    whole[:, columns_of(0, 1)] = nothing
    whole[:, columns_of(blocks + 1, 1)] = nothing

    def ahead_lane(now, later):
        return jnp.where(last_lane, pltpu.roll(later, LANES - 1, 1), pltpu.roll(now, LANES - 1, 1))

    def initial(f, comp, z, at):
        return ratio[z, :, at] * drive[f * fields + comp * layers + z, :, at]

    def swept(f, comp, z, at):
        return first[f * fields + comp * layers + z, :, at]

    def pack(value, step, j):
        at, later = block_at(j), block_at(j + 1)
        for f in range(2):
            x_here = [value(f, 0, z, at) for z in range(layers)]
            for z in range(layers):
                ex, ey, ez = x_here[z], value(f, 1, z, at), value(f, 2, z, at)
                gy = ey + (ahead_lane(ex, value(f, 0, z, later)) - ex)
                gz = ez + (x_here[z + 1] - ex) if z + 1 < layers else ez - ex
                k = f * 2 * layers + z
                out_right[step, k : k + 1, at] = gy[7:8]
                out_right[step, k + layers : k + layers + 1, at] = gz[7:8]
                out_left[step, k : k + 1, at] = ey[0:1]
                out_left[step, k + layers : k + layers + 1, at] = ez[0:1]

    def sweep(value, step, j, emit):
        at, later = block_at(j), block_at(j + 1)
        e = {}

        def get(f, comp, z):
            if (f, comp, z) not in e:
                e[f, comp, z] = value(f, comp, z, at)
            return e[f, comp, z]

        def spread(ref, k):
            return jnp.broadcast_to(ref[step, k : k + 1, at], (8, LANES))

        below = [None, None]
        for z in range(layers):
            r = ratio[z, :, at]
            s = 0.5 + 4.0 * r
            fresh = []
            for f in range(2):
                ex, ey, ez = get(f, 0, z), get(f, 1, z), get(f, 2, z)
                k = f * 2 * layers + z
                ex_y = ahead_lane(ex, value(f, 0, z, later))
                ez_y = ahead_lane(ez, value(f, 2, z, later))
                ey_x = jnp.where(last_row, spread(in_right, k), pltpu.roll(ey, 7, 0))
                ez_x = jnp.where(last_row, spread(in_right, k + layers), pltpu.roll(ez, 7, 0))
                if z + 1 < layers:
                    hx = (ez_y - ez) - (get(f, 1, z + 1) - ey)
                    hy = (get(f, 0, z + 1) - ex) - (ez_x - ez)
                else:
                    hx = (ez_y - ez) + ey
                    hy = (ez - ex) - ez_x
                hz = (ey_x - ey) - (ex_y - ex)
                hx_roll, hz_roll = pltpu.roll(hx, 1, 1), pltpu.roll(hz, 1, 1)
                hx_y = jnp.where(first_lane, carry[0, f * layers + z], hx_roll)
                hz_y = jnp.where(first_lane, carry[1, f * layers + z], hz_roll)
                carry[0, f * layers + z] = hx_roll
                carry[1, f * layers + z] = hz_roll
                hz_x = jnp.where(first_row, ey - spread(in_left, k), pltpu.roll(hz, 1, 0))
                hy_x = jnp.where(first_row, spread(in_left, k + layers) - ez, pltpu.roll(hy, 1, 0))
                cx = (hz - hz_y) - (hy if z == 0 else hy - below[f][1])
                cy = (hx if z == 0 else hx - below[f][0]) - (hz - hz_x)
                cz = (hy - hy_x) - (hx - hx_y)
                below[f] = (hx, hy)
                base = f * fields + z
                fresh.append(
                    [
                        s * here + r * (drive[base + comp * layers, :, at] - curl)
                        for comp, (here, curl) in enumerate(((ex, cx), (ey, cy), (ez, cz)))
                    ]
                )
            emit(z, at, fresh)

    def over(start, stop, step_of):
        def turn(j, state):
            step_of(j)
            return state

        lax.fori_loop(start, stop, turn, 0)

    def halo_copies(step, c, span):
        at = columns_of(span[0], span[1] - span[0])
        return [
            pltpu.make_async_remote_copy(
                src_ref=source.at[step, :, at],
                dst_ref=target.at[step, :, at],
                send_sem=halo_send.at[step, side, c],
                recv_sem=halo_recv.at[step, side, c],
                device_id=(wave, device),
                device_id_type=MESH,
            )
            for side, source, target, device in (
                (0, out_right, in_left, after),
                (1, out_left, in_right, before),
            )
        ]

    spans = [windows(blocks, chunks, 1), windows(blocks, chunks, 2)]
    copies = [[halo_copies(step, c, spans[step][c]) for c in range(chunks)] for step in range(2)]

    def arrive(step, c):
        for copy in copies[step][c]:
            copy.wait_recv()
        lo, hi = spans[step][c]
        at = columns_of(lo, hi - lo)

        @pl.when(brick == 0)
        def _():
            in_left[step, :, at] = jnp.zeros((4 * layers, (hi - lo) * LANES), jnp.float32)

        @pl.when(brick == n_brick - 1)
        def _():
            in_right[step, :, at] = jnp.zeros((4 * layers, (hi - lo) * LANES), jnp.float32)

    def set_ratio(j):
        at = block_at(j)
        for z in range(layers):
            ratio[z, :, at] = 0.5 / (4.0 + wave_sq * permit[z, :, at])

    for c in range(chunks):
        for copy in loads[c]:
            copy.wait()
        over(per * c, per * (c + 1), set_ratio)
        over(*spans[0][c], functools.partial(pack, initial, 0))
        if c == 0:
            pl.semaphore_wait(barrier, 3 * n_wave - 1)
        for copy in copies[0][c]:
            copy.start()

    def keep(z, at, fresh):
        for f in range(2):
            for comp in range(3):
                first[f * fields + comp * layers + z, :, at] = fresh[f][comp]

    def sweep_first(j):
        sweep(initial, 0, j, keep)

    carry[...] = jnp.zeros_like(carry)
    for c in range(chunks):
        arrive(0, c)
        over(*spans[0][c], sweep_first)
        over(*spans[1][c], functools.partial(pack, swept, 1))
        for copy in copies[1][c]:
            copy.start()

    def sweep_second(j):
        total = []

        def add(z, at, fresh):
            product = sum(fresh[0][comp] * fresh[1][comp] for comp in range(3))
            total[:] = [product if z == 0 else total[0] + product]

        sweep(swept, 1, j, add)
        at = block_at(j)
        mine = -wave_sq * total[0]
        density[:, at] = mine
        owner, place = j // owned, lax.rem(j, owned) * 2
        edge_top[owner, pl.ds(place, 2), :] = mine[0:2]
        edge_bottom[owner, pl.ds(place, 2), :] = mine[6:8]

    carry[...] = jnp.zeros_like(carry)
    for c in range(chunks):
        arrive(1, c)
        over(*spans[1][c], sweep_second)

    def owner_columns(w):
        return pl.ds(pl.multiple_of(w * owned * LANES, LANES), owned * LANES)

    exchanges = []
    for p in range(n_wave):
        for side, source, target, device in (
            (0, edge_bottom, from_left, after),
            (1, edge_top, from_right, before),
        ):
            exchanges.append(
                pltpu.make_async_remote_copy(
                    src_ref=source.at[peers[p]],
                    dst_ref=target.at[p],
                    send_sem=edge_send.at[side, p],
                    recv_sem=edge_recv.at[side, p],
                    device_id=(peers[p], device),
                    device_id_type=MESH,
                )
            )
        if p:
            exchanges.append(
                pltpu.make_async_remote_copy(
                    src_ref=density.at[:, owner_columns(peers[p])],
                    dst_ref=parts.at[p - 1],
                    send_sem=part_send.at[p - 1],
                    recv_sem=part_recv.at[p - 1],
                    device_id=(peers[p], brick),
                    device_id_type=MESH,
                )
            )
    for copy in exchanges:
        copy.start()
    for copy in exchanges:
        copy.wait_recv()

    total = density[:, owner_columns(wave)]
    for p in range(n_wave - 1):
        total = total + parts[p]
    left, right = from_left[0], from_right[0]
    for p in range(1, n_wave):
        left = left + from_left[p]
        right = right + from_right[p]
    left = jnp.where(brick == 0, 0.0, left)
    right = jnp.where(brick == n_brick - 1, 0.0, right)
    rows[8:16, :] = total
    for k in range(owned):
        at = columns_of(k, 1)
        rows[6:8, at] = left[2 * k : 2 * k + 2]
        rows[16:18, at] = right[2 * k : 2 * k + 2]
    mixed = WEIGHTS[0] * rows[8:16, :]
    for d in (1, 2):
        mixed = mixed + WEIGHTS[d] * (rows[8 - d : 16 - d, :] + rows[8 + d : 16 + d, :])
    mine = pl.ds(pl.multiple_of((wave * owned + 1) * LANES, LANES), owned * LANES)
    whole[:, mine] = mixed

    gathers = [
        pltpu.make_async_remote_copy(
            src_ref=whole.at[:, mine],
            dst_ref=whole.at[:, mine],
            send_sem=gather_send.at[p - 1],
            recv_sem=gather_recv.at[p - 1],
            device_id=(peers[p], brick),
            device_id_type=MESH,
        )
        for p in range(1, n_wave)
    ]
    for copy in gathers:
        copy.start()
    for step in range(2):
        for c in range(chunks):
            for copy in copies[step][c]:
                copy.wait_send()
    for copy in exchanges:
        copy.wait_send()
    for p in range(1, n_wave):
        sender = lax.rem(wave + n_wave - p, n_wave)
        theirs = pl.ds(pl.multiple_of((sender * owned + 1) * LANES, LANES), owned * LANES)
        pltpu.make_async_remote_copy(
            src_ref=whole.at[:, theirs],
            dst_ref=whole.at[:, theirs],
            send_sem=gather_send.at[p - 1],
            recv_sem=gather_recv.at[p - 1],
            device_id=(peers[p], brick),
            device_id_type=MESH,
        ).wait_recv()

    def shifted(now, beside, d):
        if d > 0:
            return jnp.where(lane >= LANES - d, pltpu.roll(beside, LANES - d, 1), pltpu.roll(now, LANES - d, 1))
        return jnp.where(lane < -d, pltpu.roll(beside, -d, 1), pltpu.roll(now, -d, 1))

    for k in range(blocks):
        back, now, later = (whole[:, columns_of(k + d, 1)] for d in range(3))
        smooth = WEIGHTS[0] * now
        for d in (1, 2):
            smooth = smooth + WEIGHTS[d] * (shifted(now, later, d) + shifted(now, back, -d))
        runs[pl.ds(k, 8, stride=blocks), :] = smooth

    def pick(q, state):
        out_ref[pl.ds(q, 1), :] = runs[pl.ds(pixel_ref[0, q], 1), :]
        return state

    lax.fori_loop(0, 8 * blocks, pick, 0, unroll=16)
    for copy in gathers:
        copy.wait_send()


def on_device(n_wave, n_brick, chunks, sources, permittivity, wave_number_sq, pixel_list):
    rows, layers, length = permittivity.shape
    blocks = length // LANES
    owned = blocks // n_wave
    planes = 6 * layers
    src = sources[0].transpose(0, 2, 1, 3).reshape(planes, rows, length)
    eps = permittivity.transpose(1, 0, 2)
    vmem, dma, f32 = pltpu.VMEM, pltpu.SemaphoreType.DMA, jnp.float32
    padded = length + LANES
    picked = pl.pallas_call(
        functools.partial(body, n_wave, n_brick, blocks, layers, chunks),
        out_shape=jax.ShapeDtypeStruct((rows * blocks, RUN), f32),
        in_specs=[
            pl.BlockSpec(memory_space=pltpu.SMEM),
            pl.BlockSpec(memory_space=pltpu.SMEM),
            pl.BlockSpec(memory_space=pl.ANY),
            pl.BlockSpec(memory_space=pl.ANY),
        ],
        out_specs=pl.BlockSpec(memory_space=pltpu.VMEM),
        scratch_shapes=[
            vmem((planes, rows, padded), f32),
            vmem((layers, rows, length), f32),
            vmem((layers, rows, padded), f32),
            vmem((planes, rows, padded), f32),
            vmem((2, 2 * layers, rows, LANES), f32),
            vmem((2, 4 * layers, length), f32),
            vmem((2, 4 * layers, length), f32),
            vmem((2, 4 * layers, length), f32),
            vmem((2, 4 * layers, length), f32),
            vmem((rows, length), f32),
            vmem((n_wave, 2 * owned, LANES), f32),
            vmem((n_wave, 2 * owned, LANES), f32),
            vmem((n_wave - 1, rows, owned * LANES), f32),
            vmem((n_wave, 2 * owned, LANES), f32),
            vmem((n_wave, 2 * owned, LANES), f32),
            vmem((24, owned * LANES), f32),
            vmem((rows, length + 2 * LANES), f32),
            vmem((rows * blocks, RUN), f32),
            dma((2, chunks)),
            dma((2, 2, chunks)),
            dma((2, 2, chunks)),
            dma((n_wave - 1,)),
            dma((n_wave - 1,)),
            dma((2, n_wave)),
            dma((2, n_wave)),
            dma((n_wave - 1,)),
            dma((n_wave - 1,)),
        ],
        compiler_params=pltpu.CompilerParams(
            collective_id=0, has_side_effects=True, vmem_limit_bytes=60 * 1024 * 1024
        ),
    )(wave_number_sq, pixel_list, src, eps)
    return picked.reshape(1, rows * length)


def solution(mesh, chunks=4):
    n_wave, n_brick = mesh.shape["wave"], mesh.shape["brick"]
    return jax.shard_map(
        functools.partial(on_device, n_wave, n_brick, chunks),
        mesh=mesh,
        in_specs=(
            P("wave", None, "brick", None, None),
            P("brick", None, None),
            P("wave"),
            P("brick", None),
        ),
        out_specs=P("brick", None),
        check_vma=False,
    )
```

time: 237 us -> 54 us (0.23)
  the two profiles are of different devices: /device:TPU:30 before, /device:TPU:1 now
where the time goes in v1:
time: 54 us; the launch traced here: 53.9 us
  Pallas kernels  51.7 us (96%)
  local copies, waits for them, and re-layouts  1.57 us (3%)
  between operations  0.66 us (1%)
    pallas_call x1, Pallas kernels, on_device(): pl.pallas_call(functools.partial(body, n_wave, n_brick, blocks, layers, c...  51.7 us
    unnamed x1, local copies, waits for them, and re-layouts  1.57 us

profile of v1, /device:TPU:1, one launch (start us, length us, event | category | flops | bytes accessed | tf_op | source)
XLA Modules:
  0.0 53.9 jit_solution(16553569299160656902)
XLA Ops:
  0.7 51.7 %shard_map.46 = f32[256,128]{1,0:T(8,128)} custom-call(f32[1]{0:T(128)S(6)} %copy.6.wave_ref, s32[1,256]{1,0:T(1,128)} %pixel_ref.1, f32[36,8,4096]{2,1,0:T(8,128)} %bitcast.7, f32[6,8,4096]{2,1,0:T(8,128)} %bitcast.8), custom_call_target="tpu_custom_call" | custom-call | tf_op jit(solution)/shard_map/pallas_call | solution.py:363
  52.4 1.6 %copy.7 = f32[1,32768]{1,0:T(1,128)} copy(f32[1,32768]{1,0:T(1,128)} %bitcast.9) | data formatting | bytes 262144

commit v2 on v1

--- a/solution.py
+++ b/solution.py
@@ -57,11 +57,10 @@
         loads.append(pair)
 
     barrier = pltpu.get_barrier_semaphore()
-    for p in range(n_wave):
-        if p:
-            pl.semaphore_signal(barrier, inc=1, device_id=(peers[p], brick), device_id_type=MESH)
-        for side in (before, after):
-            pl.semaphore_signal(barrier, inc=1, device_id=(peers[p], side), device_id_type=MESH)
+    for side in (before, after):
+        pl.semaphore_signal(barrier, inc=1, device_id=(wave, side), device_id_type=MESH)
+    for p in range(1, n_wave):
+        pl.semaphore_signal(barrier, inc=1, device_id=(peers[p], brick), device_id_type=MESH)
 
     wave_sq = wave_ref[0]
     lane = lax.broadcasted_iota(jnp.int32, (8, LANES), 1)
@@ -203,8 +202,9 @@
             copy.wait()
         over(per * c, per * (c + 1), set_ratio)
         over(*spans[0][c], functools.partial(pack, initial, 0))
-        if c == 0:
-            pl.semaphore_wait(barrier, 3 * n_wave - 1)
+
+    pl.semaphore_wait(barrier, n_wave + 1)
+    for c in range(chunks):
         for copy in copies[0][c]:
             copy.start()
 

time: 54 us -> 54.5 us (level)
  no operation moved by 1% of the time
where the time goes in v2:
time: 54.5 us; the launch traced here: 54.4 us
  Pallas kernels  52.2 us (96%)
  local copies, waits for them, and re-layouts  1.57 us (3%)
  between operations  0.66 us (1%)
    pallas_call x1, Pallas kernels, on_device(): pl.pallas_call(functools.partial(body, n_wave, n_brick, blocks, layers, c...  52.2 us
    unnamed x1, local copies, waits for them, and re-layouts  1.57 us

profile of v2, /device:TPU:1, one launch (start us, length us, event | category | flops | bytes accessed | tf_op | source)
XLA Modules:
  0.0 54.4 jit_solution(12274624817799737070)
XLA Ops:
  0.7 52.2 %shard_map.46 = f32[256,128]{1,0:T(8,128)} custom-call(f32[1]{0:T(128)S(6)} %copy.6.wave_ref, s32[1,256]{1,0:T(1,128)} %pixel_ref.1, f32[36,8,4096]{2,1,0:T(8,128)} %bitcast.7, f32[6,8,4096]{2,1,0:T(8,128)} %bitcast.8), custom_call_target="tpu_custom_call" | custom-call | tf_op jit(solution)/shard_map/pallas_call | solution.py:363
  52.8 1.6 %copy.7 = f32[1,32768]{1,0:T(1,128)} copy(f32[1,32768]{1,0:T(1,128)} %bitcast.9) | data formatting | bytes 262144

commit v3 on v2

--- a/solution.py
+++ b/solution.py
@@ -151,12 +151,17 @@
                 )
             emit(z, at, fresh)
 
-    def over(start, stop, step_of):
-        def turn(j, state):
-            step_of(j)
+    def over(start, stop, step_of, unit=1):
+        turns = (stop - start) // unit
+
+        def turn(i, state):
+            for k in range(unit):
+                step_of(start + unit * i + k)
             return state
 
-        lax.fori_loop(start, stop, turn, 0)
+        lax.fori_loop(0, turns, turn, 0)
+        if unit * turns < stop - start:
+            over(start + unit * turns, stop, step_of)
 
     def halo_copies(step, c, span):
         at = columns_of(span[0], span[1] - span[0])
@@ -201,10 +206,9 @@
         for copy in loads[c]:
             copy.wait()
         over(per * c, per * (c + 1), set_ratio)
-        over(*spans[0][c], functools.partial(pack, initial, 0))
-
-    pl.semaphore_wait(barrier, n_wave + 1)
-    for c in range(chunks):
+        over(*spans[0][c], functools.partial(pack, initial, 0), 2)
+        if c == 0:
+            pl.semaphore_wait(barrier, n_wave + 1)
         for copy in copies[0][c]:
             copy.start()
 
@@ -219,8 +223,8 @@
     carry[...] = jnp.zeros_like(carry)
     for c in range(chunks):
         arrive(0, c)
-        over(*spans[0][c], sweep_first)
-        over(*spans[1][c], functools.partial(pack, swept, 1))
+        over(*spans[0][c], sweep_first, 2)
+        over(*spans[1][c], functools.partial(pack, swept, 1), 2)
         for copy in copies[1][c]:
             copy.start()
 
@@ -235,100 +239,103 @@
         at = block_at(j)
         mine = -wave_sq * total[0]
         density[:, at] = mine
-        owner, place = j // owned, lax.rem(j, owned) * 2
-        edge_top[owner, pl.ds(place, 2), :] = mine[0:2]
-        edge_bottom[owner, pl.ds(place, 2), :] = mine[6:8]
+        edge_top[j] = mine[0:2]
+        edge_bottom[j] = mine[6:8]
+
+    def exchange(g):
+        made = []
+        for p in range(n_wave):
+            b = n_wave * g + peers[p]
+            for side, source, target, device in (
+                (0, edge_bottom, from_left, after),
+                (1, edge_top, from_right, before),
+            ):
+                made.append(
+                    pltpu.make_async_remote_copy(
+                        src_ref=source.at[b],
+                        dst_ref=target.at[g, p],
+                        send_sem=edge_send.at[side, g, p],
+                        recv_sem=edge_recv.at[side, g, p],
+                        device_id=(peers[p], device),
+                        device_id_type=MESH,
+                    )
+                )
+            if p:
+                made.append(
+                    pltpu.make_async_remote_copy(
+                        src_ref=density.at[:, block_at(b)],
+                        dst_ref=parts.at[g, p - 1],
+                        send_sem=part_send.at[g, p - 1],
+                        recv_sem=part_recv.at[g, p - 1],
+                        device_id=(peers[p], brick),
+                        device_id_type=MESH,
+                    )
+                )
+        return made
+
+    def gather(g, owner):
+        at = block_at(n_wave * g + owner + 1)
+        return [
+            pltpu.make_async_remote_copy(
+                src_ref=whole.at[:, at],
+                dst_ref=whole.at[:, at],
+                send_sem=gather_send.at[g, p - 1],
+                recv_sem=gather_recv.at[g, p - 1],
+                device_id=(peers[p], brick),
+                device_id_type=MESH,
+            )
+            for p in range(1, n_wave)
+        ]
+
+    exchanges = [exchange(g) for g in range(owned)]
+    gathers = [gather(g, wave) for g in range(owned)]
+
+    def finish(g):
+        for copy in exchanges[g]:
+            copy.wait_recv()
+        total = density[:, block_at(n_wave * g + wave)]
+        for p in range(n_wave - 1):
+            total = total + parts[g, p]
+        left, right = from_left[g, 0], from_right[g, 0]
+        for p in range(1, n_wave):
+            left = left + from_left[g, p]
+            right = right + from_right[g, p]
+        rows[8:16, :] = total
+        rows[6:8, :] = jnp.where(brick == 0, 0.0, left)
+        rows[16:18, :] = jnp.where(brick == n_brick - 1, 0.0, right)
+        mixed = WEIGHTS[0] * rows[8:16, :]
+        for d in (1, 2):
+            mixed = mixed + WEIGHTS[d] * (rows[8 - d : 16 - d, :] + rows[8 + d : 16 + d, :])
+        whole[:, block_at(n_wave * g + wave + 1)] = mixed
+        for copy in gathers[g]:
+            copy.start()
 
     carry[...] = jnp.zeros_like(carry)
+    begun = done = 0
     for c in range(chunks):
         arrive(1, c)
-        over(*spans[1][c], sweep_second)
-
-    def owner_columns(w):
-        return pl.ds(pl.multiple_of(w * owned * LANES, LANES), owned * LANES)
-
-    exchanges = []
-    for p in range(n_wave):
-        for side, source, target, device in (
-            (0, edge_bottom, from_left, after),
-            (1, edge_top, from_right, before),
-        ):
-            exchanges.append(
-                pltpu.make_async_remote_copy(
-                    src_ref=source.at[peers[p]],
-                    dst_ref=target.at[p],
-                    send_sem=edge_send.at[side, p],
-                    recv_sem=edge_recv.at[side, p],
-                    device_id=(peers[p], device),
-                    device_id_type=MESH,
-                )
-            )
-        if p:
-            exchanges.append(
-                pltpu.make_async_remote_copy(
-                    src_ref=density.at[:, owner_columns(peers[p])],
-                    dst_ref=parts.at[p - 1],
-                    send_sem=part_send.at[p - 1],
-                    recv_sem=part_recv.at[p - 1],
-                    device_id=(peers[p], brick),
-                    device_id_type=MESH,
-                )
-            )
-    for copy in exchanges:
-        copy.start()
-    for copy in exchanges:
-        copy.wait_recv()
-
-    total = density[:, owner_columns(wave)]
-    for p in range(n_wave - 1):
-        total = total + parts[p]
-    left, right = from_left[0], from_right[0]
-    for p in range(1, n_wave):
-        left = left + from_left[p]
-        right = right + from_right[p]
-    left = jnp.where(brick == 0, 0.0, left)
-    right = jnp.where(brick == n_brick - 1, 0.0, right)
-    rows[8:16, :] = total
-    for k in range(owned):
-        at = columns_of(k, 1)
-        rows[6:8, at] = left[2 * k : 2 * k + 2]
-        rows[16:18, at] = right[2 * k : 2 * k + 2]
-    mixed = WEIGHTS[0] * rows[8:16, :]
-    for d in (1, 2):
-        mixed = mixed + WEIGHTS[d] * (rows[8 - d : 16 - d, :] + rows[8 + d : 16 + d, :])
-    mine = pl.ds(pl.multiple_of((wave * owned + 1) * LANES, LANES), owned * LANES)
-    whole[:, mine] = mixed
-
-    gathers = [
-        pltpu.make_async_remote_copy(
-            src_ref=whole.at[:, mine],
-            dst_ref=whole.at[:, mine],
-            send_sem=gather_send.at[p - 1],
-            recv_sem=gather_recv.at[p - 1],
-            device_id=(peers[p], brick),
-            device_id_type=MESH,
-        )
-        for p in range(1, n_wave)
-    ]
-    for copy in gathers:
-        copy.start()
+        over(*spans[1][c], sweep_second, 2)
+        while begun < owned and spans[1][c][1] >= n_wave * (begun + 1):
+            for copy in exchanges[begun]:
+                copy.start()
+            begun += 1
+        if c >= chunks - 2 and done < begun - 2:
+            finish(done)
+            done += 1
+    for g in range(done, owned):
+        finish(g)
+
     for step in range(2):
         for c in range(chunks):
             for copy in copies[step][c]:
                 copy.wait_send()
-    for copy in exchanges:
-        copy.wait_send()
-    for p in range(1, n_wave):
-        sender = lax.rem(wave + n_wave - p, n_wave)
-        theirs = pl.ds(pl.multiple_of((sender * owned + 1) * LANES, LANES), owned * LANES)
-        pltpu.make_async_remote_copy(
-            src_ref=whole.at[:, theirs],
-            dst_ref=whole.at[:, theirs],
-            send_sem=gather_send.at[p - 1],
-            recv_sem=gather_recv.at[p - 1],
-            device_id=(peers[p], brick),
-            device_id_type=MESH,
-        ).wait_recv()
+    for g in range(owned):
+        for copy in exchanges[g]:
+            copy.wait_send()
+    for g in range(owned):
+        for p in range(1, n_wave):
+            sender = lax.rem(wave + n_wave - p, n_wave)
+            gather(g, sender)[p - 1].wait_recv()
 
     def shifted(now, beside, d):
         if d > 0:
@@ -347,8 +354,9 @@
         return state
 
     lax.fori_loop(0, 8 * blocks, pick, 0, unroll=16)
-    for copy in gathers:
-        copy.wait_send()
+    for g in range(owned):
+        for copy in gathers[g]:
+            copy.wait_send()
 
 
 def on_device(n_wave, n_brick, chunks, sources, permittivity, wave_number_sq, pixel_list):
@@ -381,23 +389,23 @@
             vmem((2, 4 * layers, length), f32),
             vmem((2, 4 * layers, length), f32),
             vmem((rows, length), f32),
-            vmem((n_wave, 2 * owned, LANES), f32),
-            vmem((n_wave, 2 * owned, LANES), f32),
-            vmem((n_wave - 1, rows, owned * LANES), f32),
-            vmem((n_wave, 2 * owned, LANES), f32),
-            vmem((n_wave, 2 * owned, LANES), f32),
-            vmem((24, owned * LANES), f32),
+            vmem((blocks, 2, LANES), f32),
+            vmem((blocks, 2, LANES), f32),
+            vmem((owned, n_wave - 1, rows, LANES), f32),
+            vmem((owned, n_wave, 2, LANES), f32),
+            vmem((owned, n_wave, 2, LANES), f32),
+            vmem((24, LANES), f32),
             vmem((rows, length + 2 * LANES), f32),
             vmem((rows * blocks, RUN), f32),
             dma((2, chunks)),
             dma((2, 2, chunks)),
             dma((2, 2, chunks)),
-            dma((n_wave - 1,)),
-            dma((n_wave - 1,)),
-            dma((2, n_wave)),
-            dma((2, n_wave)),
-            dma((n_wave - 1,)),
-            dma((n_wave - 1,)),
+            dma((owned, n_wave - 1)),
+            dma((owned, n_wave - 1)),
+            dma((2, owned, n_wave)),
+            dma((2, owned, n_wave)),
+            dma((owned, n_wave - 1)),
+            dma((owned, n_wave - 1)),
         ],
         compiler_params=pltpu.CompilerParams(
             collective_id=0, has_side_effects=True, vmem_limit_bytes=60 * 1024 * 1024

time: 54.5 us -> 52.7 us (0.967)
  Pallas kernels: 52.2 us -> 50.4 us
    pallas_call x1, Pallas kernels: 52.2 us -> 50.4 us  [on_device(): pl.pallas_call(functools.partial(body, n_wave, n_brick, blocks, layers, c...]
where the time goes in v3:
time: 52.7 us; the launch traced here: 52.6 us
  Pallas kernels  50.4 us (96%)
  local copies, waits for them, and re-layouts  1.57 us (3%)
  between operations  0.66 us (1%)
    pallas_call x1, Pallas kernels, on_device(): pl.pallas_call(functools.partial(body, n_wave, n_brick, blocks, layers, c...  50.4 us
    unnamed x1, local copies, waits for them, and re-layouts  1.57 us

profile of v3, /device:TPU:1, one launch (start us, length us, event | category | flops | bytes accessed | tf_op | source)
XLA Modules:
  0.0 52.6 jit_solution(14854014778879452213)
XLA Ops:
  0.7 50.4 %shard_map.46 = f32[256,128]{1,0:T(8,128)} custom-call(f32[1]{0:T(128)S(6)} %copy.6.wave_ref, s32[1,256]{1,0:T(1,128)} %pixel_ref.1, f32[36,8,4096]{2,1,0:T(8,128)} %bitcast.7, f32[6,8,4096]{2,1,0:T(8,128)} %bitcast.8), custom_call_target="tpu_custom_call" | custom-call | tf_op jit(solution)/shard_map/pallas_call | solution.py:371
  51.0 1.6 %copy.7 = f32[1,32768]{1,0:T(1,128)} copy(f32[1,32768]{1,0:T(1,128)} %bitcast.9) | data formatting | bytes 262144
